TPU v7x, 128 devices: a whole 4x4x4 slice. The times are simulated.
128 devices in a mesh: gx: 16 (over z, y_hi, core), gy: 8 (over y_lo, x).
Axes of the slice: x: 4, y: 4 (y_hi: 2, y_lo: 2; y = y_hi * 2 + y_lo), z: 4, core: 2. Of those that a mesh axis runs over, the one named last changes fastest.
Arguments:
- features: bfloat16 [16, 8, 32, 64, 256], P('gx', 'gy'), may hold values from -6 to 6
- weights: bfloat16 [27, 256, 256], replicated, may hold values from -0.078125 to 0.078125
- cotangent: bfloat16 [16, 8, 32, 64, 256], P('gx', 'gy'), may hold values from -6 to 6
- send_lists: int32 [16, 8, 8, 8], P('gx', 'gy'), may hold values from 0 to 31, as said below
- block_offset: int32 [16, 8, 108], P('gx', 'gy'), may hold values from 0 to 26, as said below
- block_input: int32 [16, 8, 108, 8], P('gx', 'gy'), may hold values from 0 to 95
- block_output: int32 [16, 8, 108, 8], P('gx', 'gy'), may hold values from 0 to 32, as said below
- block_count: int32 [16, 8], P('gx', 'gy'), may hold values from 1 to 108, as said below
Outputs:
- out_features: bfloat16 [16, 8, 32, 64, 256], P('gx', 'gy')
- feat_grad: bfloat16 [16, 8, 32, 64, 256], P('gx', 'gy')
- weight_grad: float32 [27, 256, 256], replicated
Inputs may be any that keep to these rules, and one draw needn't show every extreme that they name: `send_lists`: each of a device's 8 lists names 8 different tiles that the device holds. `block_offset`: 0 in blocks past block_count. `block_output`: 32 marks an unused pair; a device's used pairs of one offset name different tiles; the used blocks come first, grouped by offset, and blocks past block_count hold only unused pairs. `block_count`: some device uses all 108 blocks.
All inputs are finite; a program needn't handle non-finite values.
Results may differ from a plain program's by a relative error of at most 0.0029.
Values may be sent and summed in bfloat16 or wider, within the bound.
A program may use at most 128 MiB of HBM per device.

v0:
```python
import math

import jax
import jax.numpy as jnp
from jax import lax
from jax.sharding import PartitionSpec as P

DIRECTIONS = ((-1, -1), (-1, 0), (-1, 1), (0, -1), (0, 1), (1, -1), (1, 0), (1, 1))


def passed_along(x, axis, by):
    size = lax.axis_size(axis)
    pairs = [(i, i + by) for i in range(size) if 0 <= i + by < size]
    return lax.ppermute(x, axis, pairs)


def travel(packet, step_x, step_y):
    moved = packet
    if step_x != 0:
        moved = passed_along(moved, "gx", step_x)
    if step_y != 0:
        moved = passed_along(moved, "gy", step_y)
    return moved


def travel_back(packet, step_x, step_y):
    moved = packet
    if step_y != 0:
        moved = passed_along(moved.astype(jnp.bfloat16), "gy", -step_y).astype(moved.dtype)
    if step_x != 0:
        moved = passed_along(moved.astype(jnp.bfloat16), "gx", -step_x).astype(moved.dtype)
    return moved


def shards(
    features, weights, cotangent, send_lists, block_offset, block_input, block_output, block_count
):
    tiles = features[0, 0]
    tile_slots, voxels, channels = tiles.shape
    lists = send_lists[0, 0]
    halo_size = lists.shape[1]
    packets = tiles[lists]
    halo = jnp.stack(
        [travel(packets[which], pair[0], pair[1]) for which, pair in enumerate(DIRECTIONS)]
    )
    extended = jnp.concatenate([tiles, halo.reshape(8 * halo_size, voxels, channels)], axis=0)
    per_turn = 8
    block_slots = block_offset.shape[2]
    block_rows = block_input.shape[3]
    padded_slots = -(-block_slots // per_turn) * per_turn
    extra = padded_slots - block_slots
    used_blocks = block_count[0, 0]
    live = jnp.arange(padded_slots) < used_blocks
    offsets = jnp.pad(block_offset[0, 0], (0, extra))
    inputs = jnp.pad(block_input[0, 0], ((0, extra), (0, 0)))
    outputs = jnp.pad(block_output[0, 0], ((0, extra), (0, 0)), constant_values=tile_slots)
    outputs = jnp.where(live[:, None], outputs, tile_slots)
    turn_count = (used_blocks + per_turn - 1) // per_turn

    def slices(turn):
        start = turn * per_turn
        return (
            lax.dynamic_slice_in_dim(offsets, start, per_turn),
            lax.dynamic_slice_in_dim(inputs, start, per_turn),
            lax.dynamic_slice_in_dim(outputs, start, per_turn),
        )

    def forward_turn(turn, accum):
        turn_offsets, turn_inputs, turn_outputs = slices(turn)
        gathered = extended[turn_inputs.reshape(-1)].reshape(
            per_turn, block_rows * voxels, channels
        )
        product = jnp.einsum(
            "grc,gcd->grd", gathered, weights[turn_offsets], preferred_element_type=jnp.float32
        )
        return accum.at[turn_outputs.reshape(-1)].add(
            product.reshape(per_turn * block_rows, voxels, channels), mode="drop"
        )

    pre = lax.fori_loop(
        0, turn_count, forward_turn, jnp.zeros((tile_slots, voxels, channels), jnp.float32)
    )
    sigma = jax.nn.sigmoid(pre)
    out_features = (tiles.astype(jnp.float32) + pre * sigma).astype(jnp.bfloat16)
    incoming = cotangent[0, 0].astype(jnp.float32)
    pre_grad = (incoming * sigma * (1.0 + pre * (1.0 - sigma))).astype(jnp.bfloat16)
    padded_grad = jnp.concatenate(
        [pre_grad, jnp.zeros((1, voxels, channels), jnp.bfloat16)], axis=0
    )

    def backward_turn(turn, carry):
        ext_grad, weight_part = carry
        turn_offsets, turn_inputs, turn_outputs = slices(turn)
        gathered = extended[turn_inputs.reshape(-1)].reshape(
            per_turn, block_rows * voxels, channels
        )
        grads = padded_grad[turn_outputs.reshape(-1)].reshape(
            per_turn, block_rows * voxels, channels
        )
        mats = weights[turn_offsets]
        back = jnp.einsum("grd,gcd->grc", grads, mats, preferred_element_type=jnp.float32)
        ext_grad = ext_grad.at[turn_inputs.reshape(-1)].add(
            back.reshape(per_turn * block_rows, voxels, channels)
        )
        terms = jnp.einsum("grc,grd->gcd", gathered, grads, preferred_element_type=jnp.float32)
        weight_part = weight_part.at[turn_offsets].add(terms)
        return (ext_grad, weight_part)

    start = (
        jnp.zeros((tile_slots + 8 * halo_size, voxels, channels), jnp.float32),
        jnp.zeros(weights.shape, jnp.float32),
    )
    ext_grad, weight_part = lax.fori_loop(0, turn_count, backward_turn, start)
    adjoints = ext_grad[tile_slots:].reshape(8, halo_size, voxels, channels)
    returned = jnp.stack(
        [travel_back(adjoints[which], pair[0], pair[1]) for which, pair in enumerate(DIRECTIONS)]
    )
    feat_sum = incoming + ext_grad[:tile_slots]
    feat_sum = feat_sum.at[lists.reshape(-1)].add(returned.reshape(8 * halo_size, voxels, channels))
    feat_grad = feat_sum.astype(jnp.bfloat16)
    weight_total = lax.psum(weight_part, ("gx", "gy"))
    device_total = lax.axis_size("gx") * lax.axis_size("gy")
    weight_grad = weight_total / math.sqrt(voxels * tile_slots * device_total)
    return (out_features[None, None], feat_grad[None, None], weight_grad)


def solution(mesh):
    in_specs = (
        P("gx", "gy", None, None, None),
        P(),
        P("gx", "gy", None, None, None),
        P("gx", "gy", None, None),
        P("gx", "gy", None),
        P("gx", "gy", None, None),
        P("gx", "gy", None, None),
        P("gx", "gy"),
    )
    out_specs = (P("gx", "gy", None, None, None), P("gx", "gy", None, None, None), P())
    return jax.shard_map(shards, mesh=mesh, in_specs=in_specs, out_specs=out_specs, check_vma=False)
```

profile of v0, /device:TPU:1, one launch (start us, length us, event | category | flops | bytes accessed | tf_op | source)
XLA Modules:
  0.0 1027.5 jit_solution(5015731274001047856)
XLA Ops:
  62.8 279.6 %while.22 = (s32[]{:T(128)}, f32[32,64,256]{2,1,0:T(8,128)S(1)}, s32[]{:T(128)}, s32[112,8]{1,0:T(8,128)S(1)}, s32[112,8]{1,0:T(8,128)S(1)}, /*index=5*/bf16[96,...) while((s32[]{:T(128)}, f32[32,64,256]{2,1,0:T(8,128)S(1)}, ...), condition=%wide.region_2.3_spmd, body=%wide.region_0.2_spmd.sunk | while | flops 537921920 | bytes 26226740 | solution.py:80
  74.0 8.8 scatter_fusion
  94.0 8.8 scatter_fusion
  113.9 8.8 scatter_fusion
  133.9 8.8 scatter_fusion
  153.9 8.8 scatter_fusion
  173.8 8.8 scatter_fusion
  193.8 8.8 scatter_fusion
  213.8 8.8 scatter_fusion
  233.7 8.8 scatter_fusion
  253.7 8.8 scatter_fusion
  273.7 8.8 scatter_fusion
  293.7 8.8 scatter_fusion
  313.6 8.8 scatter_fusion
  353.4 480.6 %while.23 = (s32[]{:T(128)}, f32[96,64,256]{2,1,0:T(8,128)}, f32[27,256,256]{2,1,0:T(8,128)}, s32[]{:T(128)}, s32[112,8]{1,0:T(8,128)S(1)}, /*index=5*/s32[112,8...) while((s32[]{:T(128)}, f32[96,64,256]{2,1,0:T(8,128)}, ...), condition=%wide.region_6.7_spmd, body=%wide.region_3.6_spmd.sunk | while | flops 1075318144 | bytes 43008608 | solution.py:113
  361.9 13.4 %scatter_fusion.1 = f32[96,64,256]{2,1,0:T(8,128)} fusion(f32[96,64,256]{2,1,0:T(8,128)} %get-tuple-element.332, s32[64]{0:T(128)S(1)} %fusion.41, f32[64,64,256]{2,1,0:T(8,128)} %bitcast.112), kind=kCustom, calls=%fused_computation.7.clone.1 | custom fusion | flops 1048576 | bytes 12583168 | tf_op jit(solution)/shard_map/while/body/scatter-add | solution.py:102
  396.3 13.6 %scatter_fusion.1 = f32[96,64,256]{2,1,0:T(8,128)} fusion(f32[96,64,256]{2,1,0:T(8,128)} %get-tuple-element.332, s32[64]{0:T(128)S(1)} %fusion.41, f32[64,64,256]{2,1,0:T(8,128)} %bitcast.112), kind=kCustom, calls=%fused_computation.7.clone.1 | custom fusion | flops 1048576 | bytes 12583168 | tf_op jit(solution)/shard_map/while/body/scatter-add | solution.py:102
  430.6 13.6 %scatter_fusion.1 = f32[96,64,256]{2,1,0:T(8,128)} fusion(f32[96,64,256]{2,1,0:T(8,128)} %get-tuple-element.332, s32[64]{0:T(128)S(1)} %fusion.41, f32[64,64,256]{2,1,0:T(8,128)} %bitcast.112), kind=kCustom, calls=%fused_computation.7.clone.1 | custom fusion | flops 1048576 | bytes 12583168 | tf_op jit(solution)/shard_map/while/body/scatter-add | solution.py:102
  464.9 13.6 %scatter_fusion.1 = f32[96,64,256]{2,1,0:T(8,128)} fusion(f32[96,64,256]{2,1,0:T(8,128)} %get-tuple-element.332, s32[64]{0:T(128)S(1)} %fusion.41, f32[64,64,256]{2,1,0:T(8,128)} %bitcast.112), kind=kCustom, calls=%fused_computation.7.clone.1 | custom fusion | flops 1048576 | bytes 12583168 | tf_op jit(solution)/shard_map/while/body/scatter-add | solution.py:102
  499.2 13.5 %scatter_fusion.1 = f32[96,64,256]{2,1,0:T(8,128)} fusion(f32[96,64,256]{2,1,0:T(8,128)} %get-tuple-element.332, s32[64]{0:T(128)S(1)} %fusion.41, f32[64,64,256]{2,1,0:T(8,128)} %bitcast.112), kind=kCustom, calls=%fused_computation.7.clone.1 | custom fusion | flops 1048576 | bytes 12583168 | tf_op jit(solution)/shard_map/while/body/scatter-add | solution.py:102
  533.5 13.6 %scatter_fusion.1 = f32[96,64,256]{2,1,0:T(8,128)} fusion(f32[96,64,256]{2,1,0:T(8,128)} %get-tuple-element.332, s32[64]{0:T(128)S(1)} %fusion.41, f32[64,64,256]{2,1,0:T(8,128)} %bitcast.112), kind=kCustom, calls=%fused_computation.7.clone.1 | custom fusion | flops 1048576 | bytes 12583168 | tf_op jit(solution)/shard_map/while/body/scatter-add | solution.py:102
  567.9 13.6 %scatter_fusion.1 = f32[96,64,256]{2,1,0:T(8,128)} fusion(f32[96,64,256]{2,1,0:T(8,128)} %get-tuple-element.332, s32[64]{0:T(128)S(1)} %fusion.41, f32[64,64,256]{2,1,0:T(8,128)} %bitcast.112), kind=kCustom, calls=%fused_computation.7.clone.1 | custom fusion | flops 1048576 | bytes 12583168 | tf_op jit(solution)/shard_map/while/body/scatter-add | solution.py:102
  602.2 13.5 %scatter_fusion.1 = f32[96,64,256]{2,1,0:T(8,128)} fusion(f32[96,64,256]{2,1,0:T(8,128)} %get-tuple-element.332, s32[64]{0:T(128)S(1)} %fusion.41, f32[64,64,256]{2,1,0:T(8,128)} %bitcast.112), kind=kCustom, calls=%fused_computation.7.clone.1 | custom fusion | flops 1048576 | bytes 12583168 | tf_op jit(solution)/shard_map/while/body/scatter-add | solution.py:102
  636.4 13.5 %scatter_fusion.1 = f32[96,64,256]{2,1,0:T(8,128)} fusion(f32[96,64,256]{2,1,0:T(8,128)} %get-tuple-element.332, s32[64]{0:T(128)S(1)} %fusion.41, f32[64,64,256]{2,1,0:T(8,128)} %bitcast.112), kind=kCustom, calls=%fused_computation.7.clone.1 | custom fusion | flops 1048576 | bytes 12583168 | tf_op jit(solution)/shard_map/while/body/scatter-add | solution.py:102
  670.6 13.5 %scatter_fusion.1 = f32[96,64,256]{2,1,0:T(8,128)} fusion(f32[96,64,256]{2,1,0:T(8,128)} %get-tuple-element.332, s32[64]{0:T(128)S(1)} %fusion.41, f32[64,64,256]{2,1,0:T(8,128)} %bitcast.112), kind=kCustom, calls=%fused_computation.7.clone.1 | custom fusion | flops 1048576 | bytes 12583168 | tf_op jit(solution)/shard_map/while/body/scatter-add | solution.py:102
  704.8 13.5 %scatter_fusion.1 = f32[96,64,256]{2,1,0:T(8,128)} fusion(f32[96,64,256]{2,1,0:T(8,128)} %get-tuple-element.332, s32[64]{0:T(128)S(1)} %fusion.41, f32[64,64,256]{2,1,0:T(8,128)} %bitcast.112), kind=kCustom, calls=%fused_computation.7.clone.1 | custom fusion | flops 1048576 | bytes 12583168 | tf_op jit(solution)/shard_map/while/body/scatter-add | solution.py:102
  739.1 13.5 %scatter_fusion.1 = f32[96,64,256]{2,1,0:T(8,128)} fusion(f32[96,64,256]{2,1,0:T(8,128)} %get-tuple-element.332, s32[64]{0:T(128)S(1)} %fusion.41, f32[64,64,256]{2,1,0:T(8,128)} %bitcast.112), kind=kCustom, calls=%fused_computation.7.clone.1 | custom fusion | flops 1048576 | bytes 12583168 | tf_op jit(solution)/shard_map/while/body/scatter-add | solution.py:102
  773.4 13.5 %scatter_fusion.1 = f32[96,64,256]{2,1,0:T(8,128)} fusion(f32[96,64,256]{2,1,0:T(8,128)} %get-tuple-element.332, s32[64]{0:T(128)S(1)} %fusion.41, f32[64,64,256]{2,1,0:T(8,128)} %bitcast.112), kind=kCustom, calls=%fused_computation.7.clone.1 | custom fusion | flops 1048576 | bytes 12583168 | tf_op jit(solution)/shard_map/while/body/scatter-add | solution.py:102
  807.8 14.0 %scatter_fusion.1 = f32[96,64,256]{2,1,0:T(8,128)} fusion(f32[96,64,256]{2,1,0:T(8,128)} %get-tuple-element.332, s32[64]{0:T(128)S(1)} %fusion.41, f32[64,64,256]{2,1,0:T(8,128)} %bitcast.112), kind=kCustom, calls=%fused_computation.7.clone.1 | custom fusion | flops 1048576 | bytes 12583168 | tf_op jit(solution)/shard_map/while/body/scatter-add | solution.py:102
  878.0 9.9 collective-permute-done.20
  893.5 8.9 scatter_fusion.3
  903.5 110.5 %all-reduce.6.cloned.1.call-done = f32[27,256,256]{2,1,0:T(8,128)} async-done(((f32[27,256,256]{2,1,0:T(8,128)}), f32[27,256,256]{2,1,0:T(8,128)}) %all-reduce.6.cloned.1.call-update) | async-done | bytes 7077904 | tf_op jit(solution)/shard_map/psum | solution.py:121
  (475 shorter events, 577.4 us)
Async XLA Ops:
  7.2 1006.8 %all-reduce.6.cloned.1.call-start = ((), (), s32[]{:S(2)}) async-start(), calls=%async_computation | async-start | bytes 14155776 | tf_op jit(solution)/shard_map/psum | solution.py:121
  9.9 16.6 %copy-start.7 = (s32[1,1,108,8]{2,3,1,0:T(8,128)S(1)}, s32[1,1,108,8]{2,3,1,0:T(8,128)}, u32[]{:S(2)}) copy-start(s32[1,1,108,8]{2,3,1,0:T(8,128)} %param.18) | copy-start | bytes 10372
  9.9 16.8 %copy-start.8 = (s32[1,1,108,8]{2,3,1,0:T(8,128)S(1)}, s32[1,1,108,8]{2,3,1,0:T(8,128)}, u32[]{:S(2)}) copy-start(s32[1,1,108,8]{2,3,1,0:T(8,128)} %param.17) | copy-start | bytes 10372
  9.9 17.0 %copy-start.9 = (s32[1,1,108]{2,1,0:T(1,128)S(1)}, s32[1,1,108]{2,1,0:T(1,128)}, u32[]{:S(2)}) copy-start(s32[1,1,108]{2,1,0:T(1,128)} %param.16) | copy-start | bytes 1300
  11.0 14.2 %collective-permute-start = (bf16[8,64,256]{2,1,0:T(8,128)(2,1)S(1)}, bf16[8,64,256]{2,1,0:T(8,128)(2,1)S(1)}, u32[]{:S(2)}, u32[]{:S(2)}) collective-permute-start(bf16[8,64,256]{2,1,0:T(8,128)(2,1)S(1)} %get-tuple-element.160), channel_id=1, source_target_pairs={{8,0},{16,8},{24,16},{32,24},{40,32},{48,40},{56,48},{64,56},{72,6... | collective-permute-start | bytes 786440 | tf_op jit(solution)/shard_map/ppermute | solution.py:14
  14.2 22.7 %collective-permute-start.2 = (bf16[8,64,256]{2,1,0:T(8,128)(2,1)}, bf16[8,64,256]{2,1,0:T(8,128)(2,1)S(1)}, u32[]{:S(2)}, u32[]{:S(2)}) collective-permute-start(bf16[8,64,256]{2,1,0:T(8,128)(2,1)} %get-tuple-element.159), channel_id=1, source_target_pairs={{8,0},{16,8},{24,16},{32,24},{40,32},{48,40},{56,48},{64,56},{72,6... | collective-permute-start | bytes 786440 | tf_op jit(solution)/shard_map/ppermute | solution.py:14
  16.2 10.7 %collective-permute-start.3 = (bf16[8,64,256]{2,1,0:T(8,128)(2,1)}, bf16[8,64,256]{2,1,0:T(8,128)(2,1)S(1)}, u32[]{:S(2)}, u32[]{:S(2)}) collective-permute-start(bf16[8,64,256]{2,1,0:T(8,128)(2,1)} %get-tuple-element.158), channel_id=1, source_target_pairs={{8,0},{16,8},{24,16},{32,24},{40,32},{48,40},{56,48},{64,56},{72,6... | collective-permute-start | bytes 786440 | tf_op jit(solution)/shard_map/ppermute | solution.py:14
  18.1 32.9 %collective-permute-start.5 = (bf16[8,64,256]{2,1,0:T(8,128)(2,1)S(1)}, bf16[8,64,256]{2,1,0:T(8,128)(2,1)S(1)}, u32[]{:S(2)}, u32[]{:S(2)}) collective-permute-start(bf16[8,64,256]{2,1,0:T(8,128)(2,1)S(1)} %get-tuple-element.157), channel_id=1, source_target_pairs={{1,0},{2,1},{3,2},{4,3},{5,4},{6,5},{7,6},{9,8},{10,9},{11,10},{12... | collective-permute-start | bytes 786440 | tf_op jit(solution)/shard_map/ppermute | solution.py:14
  19.4 20.8 %collective-permute-start.7 = (bf16[8,64,256]{2,1,0:T(8,128)(2,1)S(1)}, bf16[8,64,256]{2,1,0:T(8,128)(2,1)S(1)}, u32[]{:S(2)}, u32[]{:S(2)}) collective-permute-start(bf16[8,64,256]{2,1,0:T(8,128)(2,1)S(1)} %get-tuple-element.155), channel_id=1, source_target_pairs={{0,8},{8,16},{16,24},{24,32},{32,40},{40,48},{48,56},{56,64},{64,7... | collective-permute-start | bytes 786440 | tf_op jit(solution)/shard_map/ppermute | solution.py:14
  25.2 8.0 collective-permute-start.1
  26.9 33.8 %copy-start = (bf16[1,1,32,64,256]{4,3,2,1,0:T(8,128)(2,1)S(1)}, bf16[1,1,32,64,256]{4,3,2,1,0:T(8,128)(2,1)}, u32[]{:S(2)}) copy-start(bf16[1,1,32,64,256]{4,3,2,1,0:T(8,128)(2,1)} %param.12) | copy-start | bytes 3145732
  26.9 17.2 %collective-permute-start.10 = (bf16[8,64,256]{2,1,0:T(8,128)(2,1)S(1)}, bf16[8,64,256]{2,1,0:T(8,128)(2,1)S(1)}, u32[]{:S(2)}, u32[]{:S(2)}) collective-permute-start(bf16[8,64,256]{2,1,0:T(8,128)(2,1)S(1)} %get-tuple-element.153), channel_id=1, source_target_pairs={{0,8},{8,16},{16,24},{24,32},{32,40},{40,48},{48,56},{56,64},{64,7... | collective-permute-start | bytes 786440 | tf_op jit(solution)/shard_map/ppermute | solution.py:14
  33.2 12.2 %collective-permute-start.4 = (bf16[8,64,256]{2,1,0:T(8,128)(2,1)S(1)}, bf16[8,64,256]{2,1,0:T(8,128)(2,1)S(1)}, u32[]{:S(2)}, u32[]{:S(2)}) collective-permute-start(bf16[8,64,256]{2,1,0:T(8,128)(2,1)S(1)} %collective-permute-done.3), channel_id=1, source_target_pairs={{0,1},{1,2},{2,3},{3,4},{4,5},{5,6},{6,7},{8,9},{9,10},{10,11},{11... | collective-permute-start | bytes 786440 | tf_op jit(solution)/shard_map/ppermute | solution.py:14
  36.9 14.1 %collective-permute-start.6 = (bf16[8,64,256]{2,1,0:T(8,128)(2,1)S(1)}, bf16[8,64,256]{2,1,0:T(8,128)(2,1)S(1)}, u32[]{:S(2)}, u32[]{:S(2)}) collective-permute-start(bf16[8,64,256]{2,1,0:T(8,128)(2,1)S(1)} %get-tuple-element.156), channel_id=1, source_target_pairs={{0,1},{1,2},{2,3},{3,4},{4,5},{5,6},{6,7},{8,9},{9,10},{10,11},{11... | collective-permute-start | bytes 786440 | tf_op jit(solution)/shard_map/ppermute | solution.py:14
  40.2 20.5 %collective-permute-start.9 = (bf16[8,64,256]{2,1,0:T(8,128)(2,1)S(1)}, bf16[8,64,256]{2,1,0:T(8,128)(2,1)S(1)}, u32[]{:S(2)}, u32[]{:S(2)}) collective-permute-start(bf16[8,64,256]{2,1,0:T(8,128)(2,1)S(1)} %get-tuple-element.154), channel_id=1, source_target_pairs={{0,8},{8,16},{16,24},{24,32},{32,40},{40,48},{48,56},{56,64},{64,7... | collective-permute-start | bytes 786440 | tf_op jit(solution)/shard_map/ppermute | solution.py:14
  44.2 10.5 %collective-permute-start.8 = (bf16[8,64,256]{2,1,0:T(8,128)(2,1)S(1)}, bf16[8,64,256]{2,1,0:T(8,128)(2,1)S(1)}, u32[]{:S(2)}, u32[]{:S(2)}) collective-permute-start(bf16[8,64,256]{2,1,0:T(8,128)(2,1)S(1)} %collective-permute-done.7), channel_id=1, source_target_pairs={{1,0},{2,1},{3,2},{4,3},{5,4},{6,5},{7,6},{9,8},{10,9},{11,10},{12... | collective-permute-start | bytes 786440 | tf_op jit(solution)/shard_map/ppermute | solution.py:14
  45.5 15.2 %collective-permute-start.11 = (bf16[8,64,256]{2,1,0:T(8,128)(2,1)S(1)}, bf16[8,64,256]{2,1,0:T(8,128)(2,1)S(1)}, u32[]{:S(2)}, u32[]{:S(2)}) collective-permute-start(bf16[8,64,256]{2,1,0:T(8,128)(2,1)S(1)} %collective-permute-done.10), channel_id=1, source_target_pairs={{0,1},{1,2},{2,3},{3,4},{4,5},{5,6},{6,7},{8,9},{9,10},{10,11},{11... | collective-permute-start | bytes 786440 | tf_op jit(solution)/shard_map/ppermute | solution.py:14
  838.5 5.5 collective-permute-start.12
  840.6 21.0 %collective-permute-start.14 = (bf16[8,64,256]{2,1,0:T(8,128)(2,1)}, bf16[8,64,256]{2,1,0:T(8,128)(2,1)S(1)}, u32[]{:S(2)}, u32[]{:S(2)}) collective-permute-start(bf16[8,64,256]{2,1,0:T(8,128)(2,1)} %get-tuple-element.149), channel_id=1, source_target_pairs={{0,8},{8,16},{16,24},{24,32},{32,40},{40,48},{48,56},{56,64},{64,7... | collective-permute-start | bytes 786440 | tf_op jit(solution)/shard_map/ppermute | solution.py:14
  842.5 9.4 copy-start.5
  842.5 14.5 %copy-start.4 = (bf16[8,64,256]{2,1,0:T(8,128)(2,1)S(1)}, bf16[8,64,256]{2,1,0:T(8,128)(2,1)}, u32[]{:S(2)}) copy-start(bf16[8,64,256]{2,1,0:T(8,128)(2,1)} %get-tuple-element.143) | copy-start | bytes 786436
  842.6 19.0 %copy-start.2 = (bf16[8,64,256]{2,1,0:T(8,128)(2,1)S(1)}, bf16[8,64,256]{2,1,0:T(8,128)(2,1)}, u32[]{:S(2)}) copy-start(bf16[8,64,256]{2,1,0:T(8,128)(2,1)} %get-tuple-element.146) | copy-start | bytes 786436
  842.6 14.5 %collective-permute-start.15 = (bf16[8,64,256]{2,1,0:T(8,128)(2,1)}, bf16[8,64,256]{2,1,0:T(8,128)(2,1)S(1)}, u32[]{:S(2)}, u32[]{:S(2)}) collective-permute-start(bf16[8,64,256]{2,1,0:T(8,128)(2,1)} %get-tuple-element.148), channel_id=1, source_target_pairs={{1,0},{2,1},{3,2},{4,3},{5,4},{6,5},{7,6},{9,8},{10,9},{11,10},{12... | collective-permute-start | bytes 786440 | tf_op jit(solution)/shard_map/ppermute | solution.py:14
  844.0 14.3 %collective-permute-start.13 = (bf16[8,64,256]{2,1,0:T(8,128)(2,1)}, bf16[8,64,256]{2,1,0:T(8,128)(2,1)S(1)}, u32[]{:S(2)}, u32[]{:S(2)}) collective-permute-start(bf16[8,64,256]{2,1,0:T(8,128)(2,1)} %collective-permute-done.12), channel_id=1, source_target_pairs={{0,8},{8,16},{16,24},{24,32},{32,40},{40,48},{48,56},{56,64},{64,7... | collective-permute-start | bytes 786440 | tf_op jit(solution)/shard_map/ppermute | solution.py:14
  848.2 29.8 %collective-permute-start.17 = (bf16[8,64,256]{2,1,0:T(8,128)(2,1)S(1)}, bf16[8,64,256]{2,1,0:T(8,128)(2,1)S(1)}, u32[]{:S(2)}, u32[]{:S(2)}) collective-permute-start(bf16[8,64,256]{2,1,0:T(8,128)(2,1)S(1)} %copy-done.3), channel_id=1, source_target_pairs={{0,1},{1,2},{2,3},{3,4},{4,5},{5,6},{6,7},{8,9},{9,10},{10,11},{11... | collective-permute-start | bytes 786440 | tf_op jit(solution)/shard_map/ppermute | solution.py:14
  852.0 14.7 %collective-permute-start.19 = (bf16[8,64,256]{2,1,0:T(8,128)(2,1)S(1)}, bf16[8,64,256]{2,1,0:T(8,128)(2,1)S(1)}, u32[]{:S(2)}, u32[]{:S(2)}) collective-permute-start(bf16[8,64,256]{2,1,0:T(8,128)(2,1)S(1)} %copy-done.5), channel_id=1, source_target_pairs={{0,1},{1,2},{2,3},{3,4},{4,5},{5,6},{6,7},{8,9},{9,10},{10,11},{11... | collective-permute-start | bytes 786440 | tf_op jit(solution)/shard_map/ppermute | solution.py:14
  857.0 12.7 %collective-permute-start.22 = (bf16[8,64,256]{2,1,0:T(8,128)(2,1)S(1)}, bf16[8,64,256]{2,1,0:T(8,128)(2,1)S(1)}, u32[]{:S(2)}, u32[]{:S(2)}) collective-permute-start(bf16[8,64,256]{2,1,0:T(8,128)(2,1)S(1)} %copy-done.4), channel_id=1, source_target_pairs={{1,0},{2,1},{3,2},{4,3},{5,4},{6,5},{7,6},{9,8},{10,9},{11,10},{12... | collective-permute-start | bytes 786440 | tf_op jit(solution)/shard_map/ppermute | solution.py:14
  858.3 17.7 %collective-permute-start.16 = (bf16[8,64,256]{2,1,0:T(8,128)(2,1)S(1)}, bf16[8,64,256]{2,1,0:T(8,128)(2,1)S(1)}, u32[]{:S(2)}, u32[]{:S(2)}) collective-permute-start(bf16[8,64,256]{2,1,0:T(8,128)(2,1)S(1)} %collective-permute-done.15), channel_id=1, source_target_pairs={{0,8},{8,16},{16,24},{24,32},{32,40},{40,48},{48,56},{56,64},{64,7... | collective-permute-start | bytes 786440 | tf_op jit(solution)/shard_map/ppermute | solution.py:14
  861.6 16.4 %collective-permute-start.18 = (bf16[8,64,256]{2,1,0:T(8,128)(2,1)S(1)}, bf16[8,64,256]{2,1,0:T(8,128)(2,1)S(1)}, u32[]{:S(2)}, u32[]{:S(2)}) collective-permute-start(bf16[8,64,256]{2,1,0:T(8,128)(2,1)S(1)} %copy-done.2), channel_id=1, source_target_pairs={{1,0},{2,1},{3,2},{4,3},{5,4},{6,5},{7,6},{9,8},{10,9},{11,10},{12... | collective-permute-start | bytes 786440 | tf_op jit(solution)/shard_map/ppermute | solution.py:14
  866.6 21.4 %collective-permute-start.21 = (bf16[8,64,256]{2,1,0:T(8,128)(2,1)S(1)}, bf16[8,64,256]{2,1,0:T(8,128)(2,1)S(1)}, u32[]{:S(2)}, u32[]{:S(2)}) collective-permute-start(bf16[8,64,256]{2,1,0:T(8,128)(2,1)S(1)} %get-tuple-element.144), channel_id=1, source_target_pairs={{8,0},{16,8},{24,16},{32,24},{40,32},{48,40},{56,48},{64,56},{72,6... | collective-permute-start | bytes 786440 | tf_op jit(solution)/shard_map/ppermute | solution.py:14
  869.7 18.2 %collective-permute-start.20 = (bf16[8,64,256]{2,1,0:T(8,128)(2,1)S(1)}, bf16[8,64,256]{2,1,0:T(8,128)(2,1)S(1)}, u32[]{:S(2)}, u32[]{:S(2)}) collective-permute-start(bf16[8,64,256]{2,1,0:T(8,128)(2,1)S(1)} %collective-permute-done.19), channel_id=1, source_target_pairs={{8,0},{16,8},{24,16},{32,24},{40,32},{48,40},{56,48},{64,56},{72,6... | collective-permute-start | bytes 786440 | tf_op jit(solution)/shard_map/ppermute | solution.py:14
  876.0 14.7 %collective-permute-start.23 = (bf16[8,64,256]{2,1,0:T(8,128)(2,1)S(1)}, bf16[8,64,256]{2,1,0:T(8,128)(2,1)S(1)}, u32[]{:S(2)}, u32[]{:S(2)}) collective-permute-start(bf16[8,64,256]{2,1,0:T(8,128)(2,1)S(1)} %collective-permute-done.22), channel_id=1, source_target_pairs={{8,0},{16,8},{24,16},{32,24},{40,32},{48,40},{56,48},{64,56},{72,6... | collective-permute-start | bytes 786440 | tf_op jit(solution)/shard_map/ppermute | solution.py:14
  (3 other events, 17.4 us)
Sparse Core Ops, SparseCore 0:
  834.2 179.7 all-reduce.5
where the time goes:
time: 1030 us
  other arithmetic  413 us (40%)
  local copies, waits for them, and re-layouts  223 us (22%)
  matrix products  167 us (16%)
  waiting for transfers between devices  145 us (14%)
  starting transfers between devices  63.8 us (6%)
  between operations  15.4 us (1%)
    scatter-add x14, other arithmetic, backward_turn(): ext_grad.at[turn_inputs.reshape(-1)]  190 us
    scatter-add x14, other arithmetic, forward_turn(): accum.at[turn_outputs.reshape(-1)]  123 us
    psum x1, waiting for transfers between devices, shards(): weight_total = lax.psum(weight_part, ('gx', 'gy'))  110 us
    scatter-add x14, other arithmetic, backward_turn(): weight_part = weight_part.at[turn_offsets].add(terms)  65.5 us
    ppermute x24, starting transfers between devices, passed_along(): return lax.ppermute(x, axis, pairs)  63.8 us
    dot_general x14, matrix products, forward_turn(): jnp.einsum('grc,gcd->grd', gathered, weights[turn_offsets], preferred_ele...  60.4 us
    dot_general x14, matrix products, backward_turn(): jnp.einsum('grd,gcd->grc', grads, mats, preferred_element_type=jnp.float32)  55 us
    gather x14, local copies, waits for them, and re-layouts, forward_turn(): extended[turn_inputs.reshape(-1)]  54.7 us
  transfers between devices with their start and end apart: 25, of which 8 were waited for; matrix products, arithmetic and copies ran while one was open for 2% of the time, Pallas kernels for 0%

commit v1 on v0

v1 whole, which is shorter than its diff:
```python
import functools
import math

import jax
import jax.numpy as jnp
from jax import lax
from jax.experimental import pallas as pl
from jax.experimental.pallas import tpu as pltpu
from jax.sharding import PartitionSpec as P

MESH = pl.DeviceIdType.MESH
DIRECTIONS = ((-1, -1), (-1, 0), (-1, 1), (0, -1), (0, 1), (1, -1), (1, 0), (1, 1))
K, T, V, C, H = 27, 32, 64, 256, 64
S = T + H
GX, GY = 16, 8
BF, F32 = jnp.bfloat16, jnp.float32
ORDERS = (("z", "x", "y"), ("x", "y", "z"), ("y", "z", "x"))
GROUPS, PER = 3, 9


def vmem():
    return pl.BlockSpec(memory_space=pltpu.VMEM)


def smem():
    return pl.BlockSpec(memory_space=pltpu.SMEM)


class Place:
    def __init__(self):
        self.i, self.j = lax.axis_index("gx"), lax.axis_index("gy")
        core = self.i % 2
        self.at = {"core": core, "x": self.j % 4, "z": self.i // 4, "y": ((self.i // 2) % 2) * 2 + self.j // 4}

    def device(self, **moved):
        c = {**self.at, **moved}
        return {"gx": c["z"] * 4 + (c["y"] // 2) * 2 + c["core"], "gy": (c["y"] % 2) * 4 + c["x"]}

    def inside(self, a, b):
        p, q = self.i + a, self.j + b
        return (p >= 0) & (p < GX) & (q >= 0) & (q < GY)

    def neighbour(self, a, b):
        return {"gx": jnp.clip(self.i + a, 0, GX - 1), "gy": jnp.clip(self.j + b, 0, GY - 1)}


def greet_neighbours(place, bar):
    count = 0
    for a, b in DIRECTIONS:
        @pl.when(place.inside(a, b))
        def _():
            pl.semaphore_signal(bar, inc=1, device_id=place.neighbour(a, b), device_id_type=MESH)

        count = count + jnp.where(place.inside(a, b), 1, 0)
    return count


def exchange_start(place, d, sign, src, dst, ssem, rsem):
    a, b = sign * DIRECTIONS[d][0], sign * DIRECTIONS[d][1]
    copy = pltpu.make_async_remote_copy(
        src_ref=src.at[d], dst_ref=dst.at[d], send_sem=ssem.at[d], recv_sem=rsem.at[d],
        device_id=place.neighbour(a, b), device_id_type=MESH)
    return copy, place.inside(a, b), place.inside(-a, -b)


def halo_kernel(lists, x, halo, pack, ssem, rsem):
    place = Place()
    bar = pltpu.get_barrier_semaphore()
    pl.semaphore_wait(bar, greet_neighbours(place, bar))
    order = (0, 2, 5, 7, 1, 6, 3, 4)
    for d in order:
        for h in range(8):
            pack[d, h] = x[lists[d, h]]
        copy, to, _ = exchange_start(place, d, 1, pack, halo, ssem, rsem)

        @pl.when(to)
        def _():
            copy.start()

    for d in order:
        copy, to, come = exchange_start(place, d, 1, pack, halo, ssem, rsem)

        @pl.when(come)
        def _():
            copy.wait_recv()

        @pl.when(jnp.logical_not(come))
        def _():
            halo[d] = jnp.zeros(halo.shape[1:], halo.dtype)

        @pl.when(to)
        def _():
            copy.wait_send()


def halo_exchange(lists, x):
    return pl.pallas_call(
        halo_kernel, out_shape=jax.ShapeDtypeStruct((8, 8, V, C), BF),
        in_specs=[smem(), vmem()], out_specs=vmem(),
        scratch_shapes=[pltpu.VMEM((8, 8, V, C), BF), pltpu.SemaphoreType.DMA((8,)), pltpu.SemaphoreType.DMA((8,))],
        name="halo",
        compiler_params=pltpu.CompilerParams(collective_id=0, has_side_effects=True, vmem_limit_bytes=32 << 20),
    )(lists, x)


def local_kernel(tab, x, halo, w, cot, outf, adj, loc, ext, pg, pre, acc):
    ext[:T] = x[...]
    ext[T:S] = halo[...]
    ext[S] = jnp.zeros((V, C), BF)
    pre[...] = jnp.zeros_like(pre)

    def forward(k, _):
        wk = w[k]
        for g in range(0, T, 8):
            rows = jnp.concatenate([ext[tab[k, g + n]] for n in range(8)], axis=0)
            pre[pl.ds(g * V, 8 * V), :] += jnp.dot(rows, wk, preferred_element_type=F32)
        return 0

    lax.fori_loop(0, K, forward, 0)

    def activate(t, _):
        p = pre[pl.ds(t * V, V), :]
        s = jax.nn.sigmoid(p)
        outf[t] = (x[t].astype(F32) + p * s).astype(BF)
        pg[pl.ds(t * V, V), :] = (cot[t].astype(F32) * s * (1.0 + p * (1.0 - s))).astype(BF)
        return 0

    lax.fori_loop(0, T, activate, 0)
    acc[...] = jnp.zeros_like(acc)

    def backward(k, _):
        wk = w[k]
        for g in range(0, T, 8):
            z = lax.dot_general(pg[pl.ds(g * V, 8 * V), :], wk, (((1,), (1,)), ((), ())), preferred_element_type=F32)
            for n in range(8):
                s = tab[k, g + n]
                acc[s] = acc[s] + z[n * V:(n + 1) * V]
        return 0

    lax.fori_loop(0, K, backward, 0)
    loc[...] = acc[:T] + cot[...].astype(F32)
    adj[...] = acc[T:S].astype(BF)


def local_part(tab, x, halo, w, cot):
    return pl.pallas_call(
        local_kernel,
        out_shape=(jax.ShapeDtypeStruct((T, V, C), BF), jax.ShapeDtypeStruct((H, V, C), BF),
                   jax.ShapeDtypeStruct((T, V, C), F32), jax.ShapeDtypeStruct((S + 1, V, C), BF),
                   jax.ShapeDtypeStruct((T * V, C), BF)),
        in_specs=[smem()] + [vmem()] * 4, out_specs=(vmem(),) * 5,
        scratch_shapes=[pltpu.VMEM((T * V, C), F32), pltpu.VMEM((S + 1, V, C), F32)],
        name="local",
        compiler_params=pltpu.CompilerParams(vmem_limit_bytes=56 << 20),
    )(tab, x, halo, w, cot)


def grad_kernel(tab, ext, pg, adj, ret, ag, wbuf, prec, sa, ra, sums_a, rb, sums_b, rc,
                hs, hr, ps, pr, as_, ar, bs, br, cs, cr, gcs, gcr, gbs, gbr, gas, gar, ges, ger):
    place = Place()
    core = place.at["core"]
    partner = place.device(core=1 - core)
    bar = pltpu.get_barrier_semaphore()
    count = greet_neighbours(place, bar)
    pl.semaphore_signal(bar, inc=1, device_id=partner, device_id_type=MESH)
    for axis in ("x", "y", "z"):
        for p in (1, 2, 3):
            pl.semaphore_signal(bar, inc=1, device_id=place.device(**{axis: (place.at[axis] + p) % 4}), device_id_type=MESH)
    pl.semaphore_wait(bar, count + 10)

    order = (0, 2, 5, 7, 1, 6, 3, 4)
    for d in order:
        copy, to, _ = exchange_start(place, d, -1, adj, ret, hs, hr)

        @pl.when(to)
        def _():
            copy.start()

    def remote(src, dst, send, recv, to):
        return pltpu.make_async_remote_copy(src_ref=src, dst_ref=dst, send_sem=send, recv_sem=recv, device_id=to, device_id_type=MESH)

    def to_partner(k):
        return remote(wbuf.at[k, pl.ds((1 - core) * 128, 128)], prec.at[k], ps.at[k], pr.at[k], partner)

    def where(g, n):
        axis = ORDERS[g][n]
        mine = place.at[axis]
        return mine, lambda p: (mine + p) % 4, lambda p: place.device(**{axis: (mine + p) % 4})

    def compute(g):
        def step(k, _):
            rows = jnp.concatenate([ext[tab[k, t]] for t in range(T)], axis=0)
            wbuf[k] = lax.dot_general(rows, pg[...], (((0,), (0,)), ((), ())), preferred_element_type=F32)
            to_partner(k).start()
            return 0

        lax.fori_loop(PER * g, PER * (g + 1), step, 0)

    def a_copy(g, p):
        return remote(sa.at[g, p - 1], ra.at[g, p - 1], as_.at[g, p - 1], ar.at[g, p - 1], where(g, 0)[2](p))

    def pack_a(g):
        mine, other, _ = where(g, 0)

        def step(n, _):
            k = PER * g + n
            to_partner(k).wait_recv()
            for p in (1, 2, 3):
                r = other(p) * 32
                sa[g, p - 1, n] = (wbuf[k, pl.ds(core * 128 + r, 32)] + prec[k, pl.ds(r, 32)]).astype(BF)
            return 0

        lax.fori_loop(0, PER, step, 0)
        for p in (1, 2, 3):
            a_copy(g, p).start()

    def b_copy(g, p):
        _, other, to = where(g, 1)
        return remote(sums_a.at[g, :, pl.ds(other(p) * 8, 8)], rb.at[g, p - 1], bs.at[g, p - 1], br.at[g, p - 1], to(p))

    def finish_a(g):
        mine = where(g, 0)[0]
        for p in (1, 2, 3):
            a_copy(g, p).wait_recv()

        def step(n, _):
            k = PER * g + n
            r = mine * 32
            total = wbuf[k, pl.ds(core * 128 + r, 32)] + prec[k, pl.ds(r, 32)]
            for p in (1, 2, 3):
                total = total + ra[g, p - 1, n].astype(F32)
            sums_a[g, n] = total
            return 0

        lax.fori_loop(0, PER, step, 0)
        for p in (1, 2, 3):
            b_copy(g, p).start()

    def c_copy(g, p):
        _, other, to = where(g, 2)
        first = jnp.minimum(other(p), 2) * 3
        return remote(sums_b.at[g, pl.ds(first, 3)], rc.at[g, p - 1], cs.at[g, p - 1], cr.at[g, p - 1], to(p)), other(p) < 3

    def finish_b(g):
        mine = where(g, 1)[0]
        for p in (1, 2, 3):
            b_copy(g, p).wait_recv()
        total = sums_a[g, :, pl.ds(mine * 8, 8)]
        for p in (1, 2, 3):
            total = total + rb[g, p - 1]
        sums_b[g] = total
        for p in (1, 2, 3):
            copy, to = c_copy(g, p)

            @pl.when(to)
            def _():
                copy.start()

    def gc_copy(g, p, owner):
        a, b, c = (where(g, n)[0] for n in range(3))
        block = ag.at[g, core, a, b, jnp.minimum(owner, 2)]
        return remote(block, block, gcs.at[g, p - 1], gcr.at[g, p - 1], where(g, 2)[2](p))

    def finish_c(g):
        a, b, c = (where(g, n)[0] for n in range(3))

        @pl.when(c < 3)
        def _():
            for p in (1, 2, 3):
                c_copy(g, p)[0].wait_recv()
            total = sums_b[g, pl.ds(jnp.minimum(c, 2) * 3, 3)]
            for p in (1, 2, 3):
                total = total + rc[g, p - 1]
            ag[g, core, a, b, jnp.minimum(c, 2)] = total.reshape(24, C).astype(BF)
            for p in (1, 2, 3):
                gc_copy(g, p, c).start()

    def gb_copy(g, p, owner):
        a = where(g, 0)[0]
        block = ag.at[g, core, a, owner]
        return remote(block, block, gbs.at[g, p - 1], gbr.at[g, p - 1], where(g, 1)[2](p))

    def gather_b(g):
        mine, other, _ = where(g, 2)
        for p in (1, 2, 3):
            owner = other(4 - p)

            @pl.when(owner < 3)
            def _():
                gc_copy(g, p, owner).wait_recv()

        for p in (1, 2, 3):
            gb_copy(g, p, where(g, 1)[0]).start()

    def ga_copy(g, p, owner):
        block = ag.at[g, core, owner]
        return remote(block, block, gas.at[g, p - 1], gar.at[g, p - 1], where(g, 0)[2](p))

    def ge_copy(g, p, half, owner):
        block = ag.at[g, half, owner]
        return remote(block, block, ges.at[g, p], ger.at[g, p], partner)

    def gather_a(g):
        other = where(g, 1)[1]
        for p in (1, 2, 3):
            gb_copy(g, p, other(4 - p)).wait_recv()
        mine = where(g, 0)[0]
        for p in (1, 2, 3):
            ga_copy(g, p, mine).start()
        ge_copy(g, 0, core, mine).start()

    def gather_core(g):
        other = where(g, 0)[1]
        for p in (1, 2, 3):
            ga_copy(g, p, other(4 - p)).wait_recv()
            ge_copy(g, p, core, other(4 - p)).start()

    compute(0)
    pack_a(0)
    compute(1)
    finish_a(0)
    pack_a(1)
    compute(2)
    finish_b(0)
    finish_a(1)
    pack_a(2)
    finish_c(0)
    finish_b(1)
    finish_a(2)
    gather_b(0)
    finish_c(1)
    finish_b(2)
    gather_a(0)
    gather_b(1)
    finish_c(2)
    gather_core(0)
    gather_a(1)
    gather_b(2)
    gather_core(1)
    gather_a(2)
    gather_core(2)

    for d in order:
        copy, to, come = exchange_start(place, d, -1, adj, ret, hs, hr)

        @pl.when(come)
        def _():
            copy.wait_recv()

        @pl.when(jnp.logical_not(come))
        def _():
            ret[d] = jnp.zeros(ret.shape[1:], ret.dtype)

        @pl.when(to)
        def _():
            copy.wait_send()

    def drain(k, _):
        to_partner(k).wait_send()
        return 0

    lax.fori_loop(0, K, drain, 0)
    for g in range(GROUPS):
        mine = [where(g, n)[0] for n in range(3)]
        for p in (1, 2, 3):
            a_copy(g, p).wait_send()
            b_copy(g, p).wait_send()
            copy, to = c_copy(g, p)

            @pl.when(to)
            def _():
                copy.wait_send()

            @pl.when(mine[2] < 3)
            def _():
                gc_copy(g, p, mine[2]).wait_send()

            gb_copy(g, p, mine[1]).wait_send()
            ga_copy(g, p, mine[0]).wait_send()
        other = where(g, 0)[1]
        for p in range(4):
            ge_copy(g, p, core, other(4 - p)).wait_send()
            ge_copy(g, p, 1 - core, other(4 - p)).wait_recv()


def grad_part(tab, ext, pg, adj):
    dma = pltpu.SemaphoreType.DMA
    return pl.pallas_call(
        grad_kernel,
        out_shape=(jax.ShapeDtypeStruct((8, 8, V, C), BF), jax.ShapeDtypeStruct((GROUPS, 2, 4, 4, 3, 24, C), BF)),
        in_specs=[smem()] + [vmem()] * 3, out_specs=(vmem(), vmem()),
        scratch_shapes=[
            pltpu.VMEM((K, C, C), F32), pltpu.VMEM((K, 128, C), F32),
            pltpu.VMEM((GROUPS, 3, PER, 32, C), BF), pltpu.VMEM((GROUPS, 3, PER, 32, C), BF),
            pltpu.VMEM((GROUPS, PER, 32, C), F32), pltpu.VMEM((GROUPS, 3, PER, 8, C), F32),
            pltpu.VMEM((GROUPS, PER, 8, C), F32), pltpu.VMEM((GROUPS, 3, 3, 8, C), F32),
            dma((8,)), dma((8,)), dma((K,)), dma((K,))]
            + [dma((GROUPS, 3))] * 12 + [dma((GROUPS, 4))] * 2,
        name="grads",
        compiler_params=pltpu.CompilerParams(collective_id=1, has_side_effects=True, vmem_limit_bytes=56 << 20),
    )(tab, ext, pg, adj)


def feat_kernel(lists, loc, ret, out, acc):
    acc[...] = loc[...]
    for d in range(8):
        def step(h, _):
            t = lists[d, h]
            acc[t] = acc[t] + ret[d, h].astype(F32)
            return 0

        lax.fori_loop(0, 8, step, 0)
    out[...] = acc[...].astype(BF)


def feat_part(lists, loc, ret):
    return pl.pallas_call(
        feat_kernel, out_shape=jax.ShapeDtypeStruct((T, V, C), BF),
        in_specs=[smem(), vmem(), vmem()], out_specs=vmem(),
        scratch_shapes=[pltpu.VMEM((T, V, C), F32)], name="feat",
        compiler_params=pltpu.CompilerParams(vmem_limit_bytes=32 << 20),
    )(lists, loc, ret)


def widen_kernel(scale, ag, out):
    for half in range(2):
        for a in range(4):
            for b in range(4):
                for n in range(3):
                    out[n, pl.ds(half * 128 + a * 32 + b * 8, 8)] = ag[0, half, a, b, 0, pl.ds(n * 8, 8)].astype(F32) * scale


def widen_part(ag, scale):
    return pl.pallas_call(
        functools.partial(widen_kernel, scale), out_shape=jax.ShapeDtypeStruct((K, C, C), F32),
        grid=(9,),
        in_specs=[pl.BlockSpec((1, 2, 4, 4, 1, 24, C), lambda n: (n // 3, 0, 0, 0, n % 3, 0, 0))],
        out_specs=pl.BlockSpec((3, C, C), lambda n: (n, 0, 0)), name="widen",
    )(ag)


def dense_plan(block_offset, block_input, block_output, block_count):
    blocks = block_offset.shape[0]
    live = jnp.arange(blocks) < block_count
    tiles = jnp.arange(T)
    hit = (block_output[:, :, None] == tiles) & live[:, None, None]
    spread = jnp.sum(jnp.where(hit, block_input[:, :, None] - S, 0), axis=1)
    mine = jnp.arange(K)[:, None] == block_offset[None, :]
    return S + jnp.sum(jnp.where(mine[:, :, None], spread[None], 0), axis=1)


def shards(features, weights, cotangent, send_lists, block_offset, block_input, block_output, block_count):
    x, cot, lists = features[0, 0], cotangent[0, 0], send_lists[0, 0]
    halo = halo_exchange(lists, x)
    tab = dense_plan(block_offset[0, 0], block_input[0, 0], block_output[0, 0], block_count[0, 0]).astype(jnp.int32)
    outf, adj, loc, ext, pg = local_part(tab, x, halo.reshape(H, V, C), weights, cot)
    ret, ag = grad_part(tab, ext, pg, adj.reshape(8, 8, V, C))
    feat = feat_part(lists, loc, ret)
    wgrad = widen_part(ag, 1.0 / math.sqrt(V * T * GX * GY))
    return outf[None, None], feat[None, None], wgrad


def solution(mesh):
    grid = P("gx", "gy")
    return jax.shard_map(shards, mesh=mesh, in_specs=(grid, P(), grid, grid, grid, grid, grid, grid),
                         out_specs=(grid, grid, P()), check_vma=False)
```

time: 1030 us -> 173 us (0.17)
  other arithmetic: 413 us -> 3.24 us
  local copies, waits for them, and re-layouts: 223 us -> 4.83 us
  matrix products: 167 us -> 0 us
  Pallas kernels: 0 us -> 163 us
  waiting for transfers between devices: 145 us -> 0 us
  starting transfers between devices: 63.8 us -> 0 us
  between operations: 15.4 us -> 1.34 us
    scatter-add x43 -> x0, other arithmetic: 388 us -> none  [the longest x14 190 us: backward_turn(): ext_grad.at[turn_inputs.reshape(-1)]]
    gather x71 -> x0, local copies, waits for them, and re-layouts: 208 us -> none  [the longest x14 54.7 us: forward_turn(): extended[turn_inputs.reshape(-1)]]
    dot_general x42 -> x0, matrix products: 167 us -> none  [the longest x14 60.4 us: forward_turn(): jnp.einsum('grc,gcd->grd', gathered, weights[turn_offsets], preferred_ele...]
    pallas_call x0 -> x5, Pallas kernels: none -> 163 us  [the longest x1 87.3 us: grad_part(): pl.pallas_call(grad_kernel, out_shape=(jax.ShapeDtypeStruct((8, 8, V, C),...]
    psum x1 -> x0, waiting for transfers between devices: 110 us -> none  [shards(): weight_total = lax.psum(weight_part, ('gx', 'gy'))]
    ppermute x24 -> x0, starting transfers between devices: 63.8 us -> none  [passed_along(): return lax.ppermute(x, axis, pairs)]
    ppermute x24 -> x0, waiting for transfers between devices: 34.1 us -> none  [passed_along(): return lax.ppermute(x, axis, pairs)]
  transfers between devices with their start and end apart: 25 -> 0, of which waited for: 8 -> 0; matrix products, arithmetic and copies ran while one was open for 2% -> 0% of each run, Pallas kernels for 0% -> 0%
where the time goes in v1:
time: 173 us; the launch traced here: 172 us
  Pallas kernels  163 us (94%)
  local copies, waits for them, and re-layouts  4.83 us (3%)
  other arithmetic  3.24 us (2%)
    pallas_call x1, Pallas kernels, grad_part(): pl.pallas_call(grad_kernel, out_shape=(jax.ShapeDtypeStruct((8, 8, V, C),...  87.3 us
    pallas_call x1, Pallas kernels, local_part(): pl.pallas_call(local_kernel, out_shape=(jax.ShapeDtypeStruct((T, V, C), B...  35.5 us
    pallas_call x1, Pallas kernels, halo_exchange(): pl.pallas_call(halo_kernel, out_shape=jax.ShapeDtypeStruct((8, 8, V, C),...  29.9 us
    pallas_call x1, Pallas kernels, widen_part(): pl.pallas_call(functools.partial(widen_kernel, scale), out_shape=jax.Shap...  7.47 us
    unnamed x12, local copies, waits for them, and re-layouts  4.83 us

profile of v1, /device:TPU:1, one launch (start us, length us, event | category | flops | bytes accessed | tf_op | source)
XLA Modules:
  0.0 172.2 jit_solution(3347323575514877430)
XLA Ops:
  1.3 0.7 iota_compare_fusion.1
  2.0 0.7 add_bitcast_fusion
  2.6 0.7 select_reduce_fusion.1
  3.4 0.6 select_reduce_fusion
  3.9 0.6 broadcast_add_fusion.tab
  4.5 0.0 copy-start.1
  4.5 1.2 copy-done.1
  5.8 0.0 copy-start.4
  5.8 0.7 copy-done.4
  6.4 29.9 %halo.1 = bf16[8,8,64,256]{3,2,1,0:T(8,128)(2,1)S(1)} custom-call(s32[8,8]{1,0:T(8,128)S(1)} %bitcast.16, bf16[32,64,256]{2,1,0:T(8,128)(2,1)S(1)} %bitcast.15), custom_call_target="tpu_custom_call" | custom-call | tf_op jit(solution)/shard_map/halo/pallas_call | solution.py:97
  36.3 0.0 copy-start
  36.4 1.3 copy-done
  37.7 35.5 %local.1 = (bf16[32,64,256]{2,1,0:T(8,128)(2,1)}, bf16[64,64,256]{2,1,0:T(8,128)(2,1)}, f32[32,64,256]{2,1,0:T(8,128)}, bf16[97,64,256]{2,1,0:T(8,128)(2,1)}, bf16[2048,256]{1,0:T(8,128)(2,1)}) custom-call(s32[27,32]{1,0:T(8,128)} %broadcast_add_fusion.tab, bf16[32,64,256]{2,1,0:T(8,128)(2,1)} %bitcast.14, bf16[64,64,256]{2,1,0:T(8,128)(2,1)} %bitcast.13, ...), custom_call_target="tpu_custom_call" | custom-call | tf_op jit(solution)/shard_map/local/pallas_call | solution.py:146
  73.2 0.0 copy-start.2
  73.2 0.0 copy-start.5
  73.2 87.3 %grads.1 = (bf16[8,8,64,256]{3,2,1,0:T(8,128)(2,1)}, bf16[3,2,4,4,3,24,256]{6,5,4,3,2,1,0:T(8,128)(2,1)}) custom-call(s32[27,32]{1,0:T(8,128)} %broadcast_add_fusion.tab, bf16[97,64,256]{2,1,0:T(8,128)(2,1)} %get-tuple-element.12.ext, bf16[2048,256]{1,0:T(8,128)(2,1)} %get-tuple-element.13.pg, bf16[8,8,64,256]{3,2,1,0:T(8,128)(2,1)} %bitcast.18), custom_call_target="tpu_custom_call" | custom-call | tf_op jit(solution)/shard_map/grads/pallas_call | solution.py:388
  160.5 0.0 copy-done.2
  160.5 0.0 copy-done.5
  160.5 0.0 copy-start.3
  160.6 1.6 copy-done.3
  162.1 2.6 %feat.1 = bf16[32,64,256]{2,1,0:T(8,128)(2,1)} custom-call(s32[8,8]{1,0:T(8,128)S(1)} %bitcast.17, f32[32,64,256]{2,1,0:T(8,128)S(1)} %copy-done.2, bf16[8,8,64,256]{3,2,1,0:T(8,128)(2,1)S(1)} %copy-done.3), custom_call_target="tpu_custom_call" | custom-call | tf_op jit(solution)/shard_map/feat/pallas_call | solution.py:417
  164.7 7.5 %widen.1 = f32[27,256,256]{2,1,0:T(8,128)} custom-call(bf16[3,2,4,4,3,24,256]{6,5,4,3,2,1,0:T(8,128)(2,1)} %get-tuple-element.16.ag), custom_call_target="tpu_custom_call" | custom-call | tf_op jit(solution)/shard_map/widen/pallas_call | solution.py:434
  (1 shorter events, 0.0 us)
Async XLA Ops:
  4.5 1.2 copy-start.1
  5.8 0.7 copy-start.4
  36.3 1.3 copy-start
  73.2 87.3 %copy-start.2 = (f32[32,64,256]{2,1,0:T(8,128)S(1)}, f32[32,64,256]{2,1,0:T(8,128)}, u32[]{:S(2)}) copy-start(f32[32,64,256]{2,1,0:T(8,128)} %get-tuple-element.11.loc) | copy-start | bytes 6291460
  73.2 87.3 %copy-start.5 = (s32[1,1,8,8]{3,2,1,0:T(8,128)S(1)}, s32[1,1,8,8]{3,2,1,0:T(8,128)}, u32[]{:S(2)}) copy-start(s32[1,1,8,8]{3,2,1,0:T(8,128)} %param.11) | copy-start | bytes 772
  160.5 1.6 copy-start.3
